TPU v7x, 32 devices: a whole 2x2x4 slice. The times are simulated.
32 devices in a mesh: sub: 8 (over z, x), blk: 4 (over y, core).
Axes of the slice: x: 2, y: 2, z: 4, core: 2. Of those that a mesh axis runs over, the one named last changes fastest.
Arguments:
- a_tiles: bfloat16 [768, 12, 128, 128], P(('sub', 'blk'))
- modes: bfloat16 [768, 16, 128], P(('sub', 'blk')), may hold values from -6 to 6
- col_tiles: int32 [768, 12], P(('sub', 'blk')), may hold values from 0 to 221, as said below
- fetch_list: int32 [32, 126], P(('sub', 'blk')), may hold values from 0 to 767, as said below
Outputs:
- prolong: bfloat16 [768, 12, 16, 128], P(('sub', 'blk'))
- coarse_diag: float32 [768, 256], P('sub')
Inputs may be any that keep to these rules, and one draw needn't show every extreme that they name: `col_tiles`: slot 0 of row tile t names t itself (its index within its group); the other slots name other tiles of the same group (values below 96) or 96 + h for entry h of the device's fetch list; every entry of a device's fetch list is named by some slot of that device's rows. `fetch_list`: A device's list is 7 blocks of 18 entries; each block names distinct tiles of one group other than the device's own, different blocks name different groups; tile i of group g has number g * 96 + i.
All inputs are finite; a program needn't handle non-finite values.
Results may differ from a plain program's by a relative error of at most 0.008.
Values may be sent and summed in bfloat16 or wider, within the bound.
No kernel may reach another device: no remote copies, remote signals or barrier semaphores. Data moves between devices by JAX's collectives and lax.ppermute only.
A program may use at most 64 MiB of HBM per device.

v0:
```python
import jax
import jax.numpy as jnp
from jax import lax
from jax.sharding import PartitionSpec as P

NEIGHBOURS = 26
damping = 2.0 / 3.0


def shards(a_tiles, modes, col_tiles, fetch_list):
    blk_count = lax.axis_size("blk")
    sub_count = lax.axis_size("sub")
    tile_dev = a_tiles.shape[0]
    slot_count = a_tiles.shape[1]
    tile_rows = a_tiles.shape[2]
    mode_count = modes.shape[1]
    group_size = tile_dev * blk_count
    ghost_count = fetch_list.shape[1]
    peer_count = min(NEIGHBOURS, sub_count - 1)
    per_peer = ghost_count // peer_count
    group_modes = lax.all_gather(modes, "blk", axis=0, tiled=True)
    wanted = fetch_list[0].reshape(peer_count, per_peer)
    owners = wanted[:, 0] // group_size
    within = wanted % group_size
    selector = (owners[:, None] == jnp.arange(sub_count, dtype=jnp.int32)[None, :]).astype(
        jnp.int32
    )
    requests = jnp.sum(selector[:, :, None] * (within + 1)[:, None, :], axis=0)
    received = lax.all_to_all(requests, "sub", split_axis=0, concat_axis=0, tiled=True)
    present = received > 0
    picked = group_modes[jnp.maximum(received - 1, 0)]
    picked = jnp.where(present[:, :, None, None], picked, jnp.zeros_like(picked))
    returned = lax.all_to_all(picked, "sub", split_axis=0, concat_axis=0, tiled=True)
    returned, received = (returned, received)
    ghosts = returned[owners].reshape(ghost_count, mode_count, tile_rows)
    lookup = jnp.concatenate([group_modes, ghosts], axis=0)
    gathered = lookup[col_tiles]
    product = jnp.einsum("tkrc,tkmc->tkmr", a_tiles, gathered, preferred_element_type=jnp.float32)
    inverse = 1.0 / jnp.diagonal(a_tiles[:, 0], axis1=1, axis2=2).astype(jnp.float32)
    leading = (jnp.arange(slot_count) == 0).astype(jnp.float32)
    prolong = (
        leading[None, :, None, None] * modes.astype(jnp.float32)[:, None]
        - damping * inverse[:, None, None, :] * product
    ).astype(jnp.bfloat16)
    partial_value = (
        jnp.einsum(
            "tkmr,tknr->tkmn", prolong.astype(jnp.float32), product, precision=lax.Precision.HIGHEST
        )
        / tile_rows
    )
    partial_value = partial_value.reshape(tile_dev * slot_count, mode_count * mode_count)
    segment = (
        col_tiles.reshape(-1)[:, None]
        == jnp.arange(group_size + ghost_count, dtype=jnp.int32)[None, :]
    ).astype(jnp.float32)
    slot_sums = jnp.dot(
        segment.T,
        partial_value,
        precision=lax.Precision.HIGHEST,
        preferred_element_type=jnp.float32,
    )
    ghost_sums = slot_sums[group_size:].reshape(peer_count, per_peer, mode_count * mode_count)
    outgoing = jnp.einsum(
        "jp,jmv->pmv", selector.astype(jnp.float32), ghost_sums, precision=lax.Precision.HIGHEST
    )
    incoming = lax.all_to_all(
        outgoing.astype(jnp.bfloat16), "sub", split_axis=0, concat_axis=0, tiled=True
    ).astype(outgoing.dtype)
    target = (
        received[:, :, None] == jnp.arange(1, group_size + 1, dtype=jnp.int32)[None, None, :]
    ).astype(jnp.float32)
    local_sum = slot_sums[:group_size] + jnp.einsum(
        "pmg,pmv->gv", target, incoming, precision=lax.Precision.HIGHEST
    )
    coarse_diag = lax.psum(local_sum.astype(jnp.bfloat16), "blk").astype(jnp.float32)
    return (prolong, coarse_diag)


def solution(mesh):
    in_specs = (
        P(("sub", "blk"), None, None, None),
        P(("sub", "blk"), None, None),
        P(("sub", "blk"), None),
        P(("sub", "blk"), None),
    )
    out_specs = (P(("sub", "blk"), None, None, None), P("sub", None))
    return jax.shard_map(shards, mesh=mesh, in_specs=in_specs, out_specs=out_specs, check_vma=False)
```

profile of v0, /device:TPU:0, one launch (start us, length us, event | category | flops | bytes accessed | tf_op | source)
XLA Modules:
  0.0 80.3 jit_solution(5689057946343639641)
XLA Ops:
  0.6 0.5 broadcast.175
  1.2 1.3 %reduce.11 = s32[126]{0:T(128)S(1)} reduce(s32[1,126]{1,0:T(1,128)} %param.7, s32[]{:T(128)} %broadcast.175), dimensions={0}, to_apply=%param.7.reduce_sub_computation.3 | reduce | bytes 1012 | tf_op args[3]
  2.5 0.1 reshape_squeeze.3
  2.6 0.2 fusion.9
  2.7 0.1 copy.36
  2.8 0.7 multiply_reduce_fusion
  3.5 7.3 %all-to-all-start = ((s32[8,1,18]{2,1,0:T(1,128)}), s32[8,1,18]{2,1,0:T(1,128)S(1)}, u32[]{:S(2)}, u32[]{:S(2)}) async-start(s32[8,1,18]{2,1,0:T(1,128)} %bitcast.4), calls=%async_computation | async-start | bytes 8192 | tf_op jit(solution)/shard_map/all_to_all | solution.py:29
  10.8 6.7 %all_gather.3 = bf16[96,16,128]{2,1,0:T(8,128)(2,1)S(1)} all-gather(bf16[24,16,128]{2,1,0:T(8,128)(2,1)} %param.5), channel_id=1, replica_groups=mesh['sub'=8,'blk'=4] {'blk'}, dimensions={0}, use_global_device_ids=true | all-gather | bytes 491520 | tf_op jit(solution)/shard_map/all_gather | solution.py:21
  17.6 0.7 gather_fusion.1
  18.3 1.0 %broadcast_select_fusion = bf16[8,18,16,128]{3,2,1,0:T(8,128)(2,1)} fusion(bf16[8,18,16,128]{3,2,1,0:T(8,128)(2,1)S(1)} %bitcast.31, pred[8,18]{1,0:T(8,128)(4,1)S(1)} %broadcast_compare_fusion), kind=kLoop, calls=%fused_computation.11 | loop fusion | flops 294912 | bytes 1179792 | tf_op jit(solution)/shard_map/jit(_where)/select_n | solution.py:32
  19.4 6.0 %all-to-all-start.1 = ((bf16[8,18,16,128]{3,2,1,0:T(8,128)(2,1)}), bf16[8,18,16,128]{3,2,1,0:T(8,128)(2,1)S(1)}, u32[]{:S(2)}, u32[]{:S(2)}) async-start(bf16[8,18,16,128]{3,2,1,0:T(8,128)(2,1)} %broadcast_select_fusion), calls=%async_computation.1 | async-start | bytes 1179648 | tf_op jit(solution)/shard_map/all_to_all | solution.py:33
  25.4 3.2 %copy.42 = bf16[24,1,128,128]{0,3,2,1:T(8,128)(2,1)} copy(bf16[24,1,128,128]{3,2,1,0:T(8,128)(2,1)S(1)} %slice-done) | data formatting | bytes 1572864
  28.6 1.9 %gather_fusion = bf16[128,24]{1,0:T(8,128)(2,1)S(1)} fusion(bf16[24,128,128]{0,2,1:T(8,128)(2,1)} %bitcast.30, s32[128]{0:T(128)S(1)} %or_bitcast_fusion), kind=kCustom, calls=%fused_computation | custom fusion | bytes 13312 | tf_op jit(solution)/shard_map/jit(diagonal)/gather | solution.py:39
  30.7 0.1 copy.39
  30.8 0.1 copy.38
  30.9 0.1 reshape.117
  31.0 0.1 eq.58
  31.1 10.7 %all-to-all-done.1 = bf16[8,18,16,128]{3,2,1,0:T(8,128)(2,1)S(1)} async-done(((bf16[8,18,16,128]{3,2,1,0:T(8,128)(2,1)}), bf16[8,18,16,128]{3,2,1,0:T(8,128)(2,1)S(1)}, u32[]{:S(2)}, u32[]{:S(2)}) %all-to-all-start.1) | async-done | bytes 589856 | tf_op jit(solution)/shard_map/all_to_all | solution.py:33
  41.8 0.6 gather_fusion.2
  42.4 0.1 pad_maximum_fusion
  42.5 1.8 %gather_fusion.3 = bf16[288,16,128]{2,1,0:T(8,128)(2,1)S(1)} fusion(bf16[222,16,128]{2,1,0:T(8,128)(2,1)S(1)} %pad_maximum_fusion, s32[1024]{0:T(1024)S(1)} %pad_clamp_fusion), kind=kCustom, calls=%fused_computation.3 | custom fusion | bytes 2360448 | tf_op jit(solution)/shard_map/gather | solution.py:37
  44.4 7.5 %subtract_convert_fusion = (bf16[24,12,16,128]{3,2,1,0:T(8,128)(2,1)S(1)}, f32[24,12,16,128]{3,2,1,0:T(8,128)S(1)}) fusion(f32[24,128]{1,0:T(8,128)S(1)} %multiply_bitcast_fusion, f32[24,16,128]{2,1,0:T(8,128)S(1)} %convert_element_type.44, f32[12]{0:T(128)S(1)} %compare_convert_fusion, bf16[24,12,16,128]{3,2,1,0:T(8,128)(2,1)S(1)} %bitcast.29, ...), kind=kOutput, calls=%fused_computation.4 | convolution fusion | flops 153354240 | bytes 14364720 | tf_op jit(solution)/shard_map/tkrc,tkmc->tkmr/dot_general | solution.py:38
  51.8 2.0 %convolution_multiply_fusion = f32[24,12,16,16]{3,2,1,0:T(8,128)S(1)} fusion(bf16[24,12,16,128]{3,2,1,0:T(8,128)(2,1)S(1)} %get-tuple-element.4, f32[24,12,16,128]{3,2,1,0:T(8,128)S(1)} %get-tuple-element.5), kind=kOutput, calls=%fused_computation.5 | convolution fusion | flops 113319936 | bytes 3833856 | tf_op jit(solution)/shard_map/tkmr,tknr->tkmn/dot_general | solution.py:46
  53.8 1.7 %reshape.91 = f32[288,256]{1,0:T(8,128)} reshape(f32[24,12,16,16]{3,2,1,0:T(8,128)S(1)} %convolution_multiply_fusion) | data formatting | bytes 589824 | tf_op jit(solution)/shard_map/reshape | solution.py:51
  55.5 1.5 %fusion.2 = f32[222,256]{1,0:T(8,128)S(1)} fusion(f32[288,256]{1,0:T(8,128)} %reshape.91, s32[288]{0:T(512)S(1)} %eq.58), kind=kOutput, calls=%fused_computation.13 | convolution fusion | flops 196475328 | bytes 523392 | tf_op jit(solution)/shard_map/dot_general | solution.py:56
  57.1 0.3 convolution_convert_fusion
  57.4 0.7 copy.41
  58.0 3.6 %all-to-all-start.2 = ((bf16[8,18,256]{2,1,0:T(8,128)(2,1)}), bf16[8,18,256]{2,1,0:T(8,128)(2,1)S(1)}, u32[]{:S(2)}, u32[]{:S(2)}) async-start(bf16[8,18,256]{2,1,0:T(8,128)(2,1)} %copy.41), calls=%async_computation.2 | async-start | bytes 196608 | tf_op jit(solution)/shard_map/all_to_all | solution.py:66
  61.7 7.1 %all-to-all-done.2 = bf16[8,18,256]{2,1,0:T(8,128)(2,1)S(1)} async-done(((bf16[8,18,256]{2,1,0:T(8,128)(2,1)}), bf16[8,18,256]{2,1,0:T(8,128)(2,1)S(1)}, u32[]{:S(2)}, u32[]{:S(2)}) %all-to-all-start.2) | async-done | bytes 73760 | tf_op jit(solution)/shard_map/all_to_all | solution.py:66
  68.8 0.3 fusion.1
  69.1 10.5 %psum.7 = bf16[96,256]{1,0:T(8,128)(2,1)S(1)} all-reduce(bf16[96,256]{1,0:T(8,128)(2,1)S(1)} %fusion.1), channel_id=1, replica_groups=mesh['sub'=8,'blk'=4] {'blk'}, use_global_device_ids=true, to_apply=%region_1.2 | all-reduce | flops 24576 | bytes 98304 | tf_op jit(solution)/shard_map/psum | solution.py:75
  79.6 0.6 convert_element_type.51
  (26 shorter events, 0.3 us)
Async XLA Ops:
  0.6 24.7 %copy-start.1 = (bf16[24,16,128]{2,1,0:T(8,128)(2,1)S(1)}, bf16[24,16,128]{2,1,0:T(8,128)(2,1)}, u32[]{:S(2)}) copy-start(bf16[24,16,128]{2,1,0:T(8,128)(2,1)} %param.5) | copy-start | bytes 294916
  3.5 14.0 %all-to-all-start = ((s32[8,1,18]{2,1,0:T(1,128)}), s32[8,1,18]{2,1,0:T(1,128)S(1)}, u32[]{:S(2)}, u32[]{:S(2)}) async-start(s32[8,1,18]{2,1,0:T(1,128)} %bitcast.4), calls=%async_computation | async-start | bytes 8192 | tf_op jit(solution)/shard_map/all_to_all | solution.py:29
  18.3 7.1 %slice-start = ((bf16[24,12,128,128]{3,2,1,0:T(8,128)(2,1)}), bf16[24,1,128,128]{3,2,1,0:T(8,128)(2,1)S(1)}, s32[]{:S(2)}) async-start(bf16[24,12,128,128]{3,2,1,0:T(8,128)(2,1)} %param.4), calls=%async_computation.3 | async-start | bytes 1572864 | tf_op jit(solution)/shard_map/slice | solution.py:39
  19.4 22.4 %all-to-all-start.1 = ((bf16[8,18,16,128]{3,2,1,0:T(8,128)(2,1)}), bf16[8,18,16,128]{3,2,1,0:T(8,128)(2,1)S(1)}, u32[]{:S(2)}, u32[]{:S(2)}) async-start(bf16[8,18,16,128]{3,2,1,0:T(8,128)(2,1)} %broadcast_select_fusion), calls=%async_computation.1 | async-start | bytes 1179648 | tf_op jit(solution)/shard_map/all_to_all | solution.py:33
  25.4 5.3 %copy-start.2 = (s32[24,12]{0,1:T(8,128)S(1)}, s32[24,12]{0,1:T(8,128)}, u32[]{:S(2)}) copy-start(s32[24,12]{0,1:T(8,128)} %param.6) | copy-start | bytes 3460
  51.8 2.0 %copy-start = (bf16[24,12,16,128]{3,2,1,0:T(8,128)(2,1)}, bf16[24,12,16,128]{3,2,1,0:T(8,128)(2,1)S(1)}, u32[]{:S(2)}) copy-start(bf16[24,12,16,128]{3,2,1,0:T(8,128)(2,1)S(1)} %get-tuple-element.4) | copy-start | bytes 3538948
  58.0 10.8 %all-to-all-start.2 = ((bf16[8,18,256]{2,1,0:T(8,128)(2,1)}), bf16[8,18,256]{2,1,0:T(8,128)(2,1)S(1)}, u32[]{:S(2)}, u32[]{:S(2)}) async-start(bf16[8,18,256]{2,1,0:T(8,128)(2,1)} %copy.41), calls=%async_computation.2 | async-start | bytes 196608 | tf_op jit(solution)/shard_map/all_to_all | solution.py:66
where the time goes:
time: 80.7 us; the launch traced here: 80.3 us
  waiting for transfers between devices  17.8 us (22%)
  blocking collectives  17.2 us (21%)
  starting transfers between devices  16.9 us (21%)
  local copies, waits for them, and re-layouts  12 us (15%)
  matrix products  11.6 us (14%)
  other arithmetic  4.03 us (5%)
  between operations  0.83 us (1%)
    all_to_all x1, waiting for transfers between devices, shards(): lax.all_to_all(picked, 'sub', split_axis=0, concat_axis=0, tiled=True)  10.7 us
    psum x1, blocking collectives, shards(): lax.psum(local_sum.astype(jnp.bfloat16), 'blk').astype(jnp.float32)  10.5 us
    dot_general x1, matrix products, shards(): jnp.einsum('tkrc,tkmc->tkmr', a_tiles, gathered, preferred_element_type=j...  7.47 us
    all_to_all x1, starting transfers between devices, shards(): lax.all_to_all(requests, 'sub', split_axis=0, concat_axis=0, tiled=True)  7.28 us
    all_to_all x1, waiting for transfers between devices, shards(): lax.all_to_all(outgoing.astype(jnp.bfloat16), 'sub', split_axis=0, concat...  7.12 us
    all_gather x1, blocking collectives, shards(): group_modes = lax.all_gather(modes, 'blk', axis=0, tiled=True)  6.68 us
    all_to_all x1, starting transfers between devices, shards(): lax.all_to_all(picked, 'sub', split_axis=0, concat_axis=0, tiled=True)  5.99 us
    unnamed x9, local copies, waits for them, and re-layouts  3.84 us
  transfers between devices with their start and end apart: 3, of which 2 were waited for; matrix products, arithmetic and copies ran while one was open for 7% of the time, Pallas kernels for 0%

commit v1 on v0

--- a/solution.py
+++ b/solution.py
@@ -72,7 +72,9 @@
     local_sum = slot_sums[:group_size] + jnp.einsum(
         "pmg,pmv->gv", target, incoming, precision=lax.Precision.HIGHEST
     )
-    coarse_diag = lax.psum(local_sum.astype(jnp.bfloat16), "blk").astype(jnp.float32)
+    coarse_diag = jnp.sum(lax.all_gather(local_sum.astype(jnp.bfloat16), "blk"), axis=0).astype(
+        jnp.float32
+    )
     return (prolong, coarse_diag)
 
 

time: 80.7 us -> 75.8 us (0.939)
  blocking collectives: 17.2 us -> 12.3 us
    psum x1 -> x0, blocking collectives: 10.5 us -> none  [shards(): lax.psum(local_sum.astype(jnp.bfloat16), 'blk').astype(jnp.float32)]
    all_gather x0 -> x1, blocking collectives: none -> 5.6 us  [shards(): lax.all_gather(local_sum.astype(jnp.bfloat16), 'blk')]
  transfers between devices with their start and end apart: 3 -> 3, of which waited for: 2 -> 2; matrix products, arithmetic and copies ran while one was open for 7% -> 8% of each run, Pallas kernels for 0% -> 0%
where the time goes in v1:
time: 75.8 us; the launch traced here: 75.4 us
  waiting for transfers between devices  17.8 us (23%)
  starting transfers between devices  16.9 us (22%)
  blocking collectives  12.3 us (16%)
  local copies, waits for them, and re-layouts  12 us (16%)
  matrix products  11.6 us (15%)
  other arithmetic  4.06 us (5%)
  between operations  0.82 us (1%)
    all_to_all x1, waiting for transfers between devices, shards(): lax.all_to_all(picked, 'sub', split_axis=0, concat_axis=0, tiled=True)  10.7 us
    dot_general x1, matrix products, shards(): jnp.einsum('tkrc,tkmc->tkmr', a_tiles, gathered, preferred_element_type=j...  7.47 us
    all_to_all x1, starting transfers between devices, shards(): lax.all_to_all(requests, 'sub', split_axis=0, concat_axis=0, tiled=True)  7.28 us
    all_to_all x1, waiting for transfers between devices, shards(): lax.all_to_all(outgoing.astype(jnp.bfloat16), 'sub', split_axis=0, concat...  7.12 us
    all_gather x1, blocking collectives, shards(): group_modes = lax.all_gather(modes, 'blk', axis=0, tiled=True)  6.68 us
    all_to_all x1, starting transfers between devices, shards(): lax.all_to_all(picked, 'sub', split_axis=0, concat_axis=0, tiled=True)  5.99 us
    all_gather x1, blocking collectives, shards(): lax.all_gather(local_sum.astype(jnp.bfloat16), 'blk')  5.6 us
    unnamed x9, local copies, waits for them, and re-layouts  3.84 us
  transfers between devices with their start and end apart: 3, of which 2 were waited for; matrix products, arithmetic and copies ran while one was open for 8% of the time, Pallas kernels for 0%

profile of v1, /device:TPU:0, one launch (start us, length us, event | category | flops | bytes accessed | tf_op | source)
XLA Modules:
  0.0 75.4 jit_solution(9529276588902708508)
XLA Ops:
  0.6 0.5 broadcast.175
  1.2 1.3 %reduce.12 = s32[126]{0:T(128)S(1)} reduce(s32[1,126]{1,0:T(1,128)} %param.7, s32[]{:T(128)} %broadcast.175), dimensions={0}, to_apply=%param.7.reduce_sub_computation.3 | reduce | bytes 1012 | tf_op args[3]
  2.5 0.1 reshape_squeeze.3
  2.6 0.2 fusion.9
  2.7 0.1 copy.36
  2.8 0.7 multiply_reduce_fusion
  3.5 7.3 %all-to-all-start = ((s32[8,1,18]{2,1,0:T(1,128)}), s32[8,1,18]{2,1,0:T(1,128)S(1)}, u32[]{:S(2)}, u32[]{:S(2)}) async-start(s32[8,1,18]{2,1,0:T(1,128)} %bitcast.4), calls=%async_computation | async-start | bytes 8192 | tf_op jit(solution)/shard_map/all_to_all | solution.py:29
  10.8 6.7 %all_gather.9 = bf16[96,16,128]{2,1,0:T(8,128)(2,1)S(1)} all-gather(bf16[24,16,128]{2,1,0:T(8,128)(2,1)} %param.5), channel_id=1, replica_groups=mesh['sub'=8,'blk'=4] {'blk'}, dimensions={0}, use_global_device_ids=true | all-gather | bytes 491520 | tf_op jit(solution)/shard_map/all_gather | solution.py:21
  17.6 0.7 gather_fusion.1
  18.3 1.0 %broadcast_select_fusion = bf16[8,18,16,128]{3,2,1,0:T(8,128)(2,1)} fusion(bf16[8,18,16,128]{3,2,1,0:T(8,128)(2,1)S(1)} %bitcast.32, pred[8,18]{1,0:T(8,128)(4,1)S(1)} %broadcast_compare_fusion), kind=kLoop, calls=%fused_computation.11 | loop fusion | flops 294912 | bytes 1179792 | tf_op jit(solution)/shard_map/jit(_where)/select_n | solution.py:32
  19.4 6.0 %all-to-all-start.1 = ((bf16[8,18,16,128]{3,2,1,0:T(8,128)(2,1)}), bf16[8,18,16,128]{3,2,1,0:T(8,128)(2,1)S(1)}, u32[]{:S(2)}, u32[]{:S(2)}) async-start(bf16[8,18,16,128]{3,2,1,0:T(8,128)(2,1)} %broadcast_select_fusion), calls=%async_computation.1 | async-start | bytes 1179648 | tf_op jit(solution)/shard_map/all_to_all | solution.py:33
  25.4 3.2 %copy.42 = bf16[24,1,128,128]{0,3,2,1:T(8,128)(2,1)} copy(bf16[24,1,128,128]{3,2,1,0:T(8,128)(2,1)S(1)} %slice-done) | data formatting | bytes 1572864
  28.6 1.9 %gather_fusion = bf16[128,24]{1,0:T(8,128)(2,1)S(1)} fusion(bf16[24,128,128]{0,2,1:T(8,128)(2,1)} %bitcast.31, s32[128]{0:T(128)S(1)} %or_bitcast_fusion), kind=kCustom, calls=%fused_computation | custom fusion | bytes 13312 | tf_op jit(solution)/shard_map/jit(diagonal)/gather | solution.py:39
  30.7 0.1 copy.39
  30.8 0.1 copy.38
  30.9 0.1 reshape.117
  31.0 0.1 eq.58
  31.1 10.7 %all-to-all-done.1 = bf16[8,18,16,128]{3,2,1,0:T(8,128)(2,1)S(1)} async-done(((bf16[8,18,16,128]{3,2,1,0:T(8,128)(2,1)}), bf16[8,18,16,128]{3,2,1,0:T(8,128)(2,1)S(1)}, u32[]{:S(2)}, u32[]{:S(2)}) %all-to-all-start.1) | async-done | bytes 589856 | tf_op jit(solution)/shard_map/all_to_all | solution.py:33
  41.8 0.6 gather_fusion.2
  42.4 0.1 pad_maximum_fusion
  42.5 1.8 %gather_fusion.3 = bf16[288,16,128]{2,1,0:T(8,128)(2,1)S(1)} fusion(bf16[222,16,128]{2,1,0:T(8,128)(2,1)S(1)} %pad_maximum_fusion, s32[1024]{0:T(1024)S(1)} %pad_clamp_fusion), kind=kCustom, calls=%fused_computation.3 | custom fusion | bytes 2360448 | tf_op jit(solution)/shard_map/gather | solution.py:37
  44.4 7.5 %subtract_convert_fusion = (bf16[24,12,16,128]{3,2,1,0:T(8,128)(2,1)S(1)}, f32[24,12,16,128]{3,2,1,0:T(8,128)S(1)}) fusion(f32[24,128]{1,0:T(8,128)S(1)} %multiply_bitcast_fusion, f32[24,16,128]{2,1,0:T(8,128)S(1)} %convert_element_type.46, f32[12]{0:T(128)S(1)} %compare_convert_fusion, bf16[24,12,16,128]{3,2,1,0:T(8,128)(2,1)S(1)} %bitcast.30, ...), kind=kOutput, calls=%fused_computation.4 | convolution fusion | flops 153354240 | bytes 14364720 | tf_op jit(solution)/shard_map/tkrc,tkmc->tkmr/dot_general | solution.py:38
  51.8 2.0 %convolution_multiply_fusion = f32[24,12,16,16]{3,2,1,0:T(8,128)S(1)} fusion(bf16[24,12,16,128]{3,2,1,0:T(8,128)(2,1)S(1)} %get-tuple-element.4, f32[24,12,16,128]{3,2,1,0:T(8,128)S(1)} %get-tuple-element.5), kind=kOutput, calls=%fused_computation.5 | convolution fusion | flops 113319936 | bytes 3833856 | tf_op jit(solution)/shard_map/tkmr,tknr->tkmn/dot_general | solution.py:46
  53.8 1.7 %reshape.91 = f32[288,256]{1,0:T(8,128)} reshape(f32[24,12,16,16]{3,2,1,0:T(8,128)S(1)} %convolution_multiply_fusion) | data formatting | bytes 589824 | tf_op jit(solution)/shard_map/reshape | solution.py:51
  55.5 1.5 %fusion.2 = f32[222,256]{1,0:T(8,128)S(1)} fusion(f32[288,256]{1,0:T(8,128)} %reshape.91, s32[288]{0:T(512)S(1)} %eq.58), kind=kOutput, calls=%fused_computation.13 | convolution fusion | flops 196475328 | bytes 523392 | tf_op jit(solution)/shard_map/dot_general | solution.py:56
  57.1 0.3 convolution_convert_fusion
  57.4 0.7 copy.41
  58.0 3.6 %all-to-all-start.2 = ((bf16[8,18,256]{2,1,0:T(8,128)(2,1)}), bf16[8,18,256]{2,1,0:T(8,128)(2,1)S(1)}, u32[]{:S(2)}, u32[]{:S(2)}) async-start(bf16[8,18,256]{2,1,0:T(8,128)(2,1)} %copy.41), calls=%async_computation.2 | async-start | bytes 196608 | tf_op jit(solution)/shard_map/all_to_all | solution.py:66
  61.7 7.1 %all-to-all-done.2 = bf16[8,18,256]{2,1,0:T(8,128)(2,1)S(1)} async-done(((bf16[8,18,256]{2,1,0:T(8,128)(2,1)}), bf16[8,18,256]{2,1,0:T(8,128)(2,1)S(1)}, u32[]{:S(2)}, u32[]{:S(2)}) %all-to-all-start.2) | async-done | bytes 73760 | tf_op jit(solution)/shard_map/all_to_all | solution.py:66
  68.8 0.3 fusion.1
  69.1 5.6 %all-gather = bf16[384,256]{1,0:T(8,128)(2,1)S(1)} all-gather(bf16[96,256]{1,0:T(8,128)(2,1)S(1)} %fusion.1), channel_id=2, replica_groups=mesh['sub'=8,'blk'=4] {'blk'}, dimensions={0}, use_global_device_ids=true | all-gather | bytes 245760 | tf_op jit(solution)/shard_map/all_gather | solution.py:75
  74.7 0.6 convert_element_type.53
  (27 shorter events, 0.3 us)
Async XLA Ops:
  0.6 24.7 %copy-start.1 = (bf16[24,16,128]{2,1,0:T(8,128)(2,1)S(1)}, bf16[24,16,128]{2,1,0:T(8,128)(2,1)}, u32[]{:S(2)}) copy-start(bf16[24,16,128]{2,1,0:T(8,128)(2,1)} %param.5) | copy-start | bytes 294916
  3.5 14.0 %all-to-all-start = ((s32[8,1,18]{2,1,0:T(1,128)}), s32[8,1,18]{2,1,0:T(1,128)S(1)}, u32[]{:S(2)}, u32[]{:S(2)}) async-start(s32[8,1,18]{2,1,0:T(1,128)} %bitcast.4), calls=%async_computation | async-start | bytes 8192 | tf_op jit(solution)/shard_map/all_to_all | solution.py:29
  18.3 7.1 %slice-start = ((bf16[24,12,128,128]{3,2,1,0:T(8,128)(2,1)}), bf16[24,1,128,128]{3,2,1,0:T(8,128)(2,1)S(1)}, s32[]{:S(2)}) async-start(bf16[24,12,128,128]{3,2,1,0:T(8,128)(2,1)} %param.4), calls=%async_computation.3 | async-start | bytes 1572864 | tf_op jit(solution)/shard_map/slice | solution.py:39
  19.4 22.4 %all-to-all-start.1 = ((bf16[8,18,16,128]{3,2,1,0:T(8,128)(2,1)}), bf16[8,18,16,128]{3,2,1,0:T(8,128)(2,1)S(1)}, u32[]{:S(2)}, u32[]{:S(2)}) async-start(bf16[8,18,16,128]{3,2,1,0:T(8,128)(2,1)} %broadcast_select_fusion), calls=%async_computation.1 | async-start | bytes 1179648 | tf_op jit(solution)/shard_map/all_to_all | solution.py:33
  25.4 5.3 %copy-start.2 = (s32[24,12]{0,1:T(8,128)S(1)}, s32[24,12]{0,1:T(8,128)}, u32[]{:S(2)}) copy-start(s32[24,12]{0,1:T(8,128)} %param.6) | copy-start | bytes 3460
  51.8 2.0 %copy-start = (bf16[24,12,16,128]{3,2,1,0:T(8,128)(2,1)}, bf16[24,12,16,128]{3,2,1,0:T(8,128)(2,1)S(1)}, u32[]{:S(2)}) copy-start(bf16[24,12,16,128]{3,2,1,0:T(8,128)(2,1)S(1)} %get-tuple-element.4) | copy-start | bytes 3538948
  58.0 10.8 %all-to-all-start.2 = ((bf16[8,18,256]{2,1,0:T(8,128)(2,1)}), bf16[8,18,256]{2,1,0:T(8,128)(2,1)S(1)}, u32[]{:S(2)}, u32[]{:S(2)}) async-start(bf16[8,18,256]{2,1,0:T(8,128)(2,1)} %copy.41), calls=%async_computation.2 | async-start | bytes 196608 | tf_op jit(solution)/shard_map/all_to_all | solution.py:66
